TPU v7x, 256 devices: a whole 4x4x8 slice. The times are simulated.
256 devices in a mesh: req: 32 (over x, y, z_lo), tp: 8 (over z_hi, core).
Axes of the slice: x: 4, y: 4, z: 8 (z_hi: 4, z_lo: 2; z = z_hi * 2 + z_lo), core: 2. Of those that a mesh axis runs over, the one named last changes fastest.
Arguments:
- hidden_in: bfloat16 [1024, 24, 3072], P(('req', 'tp')), may hold values from -6 to 6
- norm_gain: float32 [3072], replicated, may hold values from 0.1 to 1.9
- w_q: bfloat16 [3072, 3072], P(None, 'tp'), may hold values from -0.108253175 to 0.108253175
- w_k: bfloat16 [3072, 3072], P(None, 'tp'), may hold values from -3.35584844 to 3.35584844
- w_v: bfloat16 [3072, 3072], P(None, 'tp'), may hold values from -0.109375 to 0.109375
- w_o: bfloat16 [3072, 3072], P('tp'), may hold values from -0.109375 to 0.109375
- lengths: int32 [32, 32], P('req'), may hold values from 1 to 24, 576 in all within a row
- dest: int32 [32, 32, 1], P('req'), may hold values from 0 to 31; in each aligned block of 32 rows (0 to 31, 32 to 63, ..., all dimensions but the last counted through in order) at most 2 rows name the same one
Outputs:
- hidden_out: bfloat16 [1024, 24, 3072], P(('req', 'tp'))
- cache: bfloat16 [2048, 24, 2, 3072], P('req', None, None, 'tp')
Inputs may be any that keep to these rules, and one draw needn't show every extreme that they name: Each replica's lengths sum to 576 and the longest is 24. `dest`: no replica names one destination for more than 2 of its requests, and some replica names one exactly 2 times.
All inputs are finite; a program needn't handle non-finite values.
Results may differ from a plain program's by a relative error of at most 0.015.
Values may be sent and summed in bfloat16 or wider, within the bound.
No kernel may reach another device: no remote copies, remote signals or barrier semaphores. Data moves between devices by JAX's collectives and lax.ppermute only.
A program may use at most 128 MiB of HBM per device.

v0:
```python
import jax
import jax.numpy as jnp
from jax import lax
from jax.sharding import PartitionSpec as P

HD = 96
CAP = 2
EPS = 1e-05


def rope_tables(slot):
    pos = jnp.arange(slot, dtype=jnp.float32)
    inv = 10000.0 ** (-(jnp.arange(HD // 2, dtype=jnp.float32) * 2.0) / HD)
    angle = pos[:, None] * inv[None, :]
    cosine = jnp.concatenate([jnp.cos(angle), jnp.cos(angle)], -1)
    sine = jnp.concatenate([jnp.sin(angle), jnp.sin(angle)], -1)
    return (cosine, sine)


def rotate(x, cosine, sine):
    half = HD // 2
    turned = jnp.concatenate([-x[..., half:], x[..., :half]], -1)
    return x * cosine[None, :, None, :] + turned * sine[None, :, None, :]


def on_device(hidden_in, norm_gain, w_q, w_k, w_v, w_o, lengths, dest):
    req_dev, slot, width = hidden_in.shape
    req_rep = req_dev * lax.axis_size("tp")
    per_dev = w_q.shape[1]
    heads_dev = per_dev // HD
    cosine, sine = rope_tables(slot)
    xf = hidden_in.astype(jnp.float32)
    mean_sq = jnp.mean(xf * xf, -1, keepdims=True)
    normed = (xf * lax.rsqrt(mean_sq + EPS) * norm_gain).astype(jnp.bfloat16)
    piece = lax.all_gather(normed, "tp", axis=0, tiled=True)
    count = piece.shape[0]
    flat = piece.reshape(count * slot, width)
    shape4 = (count, slot, heads_dev, HD)
    query = rotate(
        jnp.dot(flat, w_q, preferred_element_type=jnp.float32).reshape(shape4), cosine, sine
    )
    keys = rotate(
        jnp.dot(flat, w_k, preferred_element_type=jnp.float32).reshape(shape4), cosine, sine
    )
    values = jnp.dot(flat, w_v, preferred_element_type=jnp.float32)
    query = query.astype(jnp.bfloat16).reshape(count, slot, per_dev)
    keys = keys.astype(jnp.bfloat16).reshape(count, slot, per_dev)
    values = values.astype(jnp.bfloat16).reshape(count, slot, per_dev)
    projected = jnp.stack([query, keys, values], 2)
    shape4 = (req_rep, slot, heads_dev, HD)
    query = projected[:, :, 0].reshape(shape4)
    keys = projected[:, :, 1]
    values = projected[:, :, 2]
    lens = lengths[0]
    live = jnp.arange(slot, dtype=jnp.int32)[None, :] < lens[:, None]
    causal = jnp.arange(slot)[None, :] <= jnp.arange(slot)[:, None]
    mask = causal[None, None, :, :] & live[:, None, None, :]
    scores = jnp.einsum(
        "rqhd,rkhd->rhqk", query, keys.reshape(shape4), preferred_element_type=jnp.float32
    ) / jnp.sqrt(jnp.float32(HD))
    scores = jnp.where(mask, scores, jnp.float32(-1e30))
    top = jnp.max(scores, -1, keepdims=True)
    expo = jnp.where(mask, jnp.exp(scores - top), 0.0)
    probs = (expo / jnp.sum(expo, -1, keepdims=True)).astype(jnp.bfloat16)
    attn = jnp.einsum(
        "rhqk,rkhd->rqhd", probs, values.reshape(shape4), preferred_element_type=jnp.float32
    )
    attn = attn.astype(jnp.bfloat16).reshape(req_rep, slot, per_dev)
    stacked = jnp.stack([keys, values], 2)
    stacked = jnp.where(live[:, :, None, None], stacked, jnp.zeros_like(stacked))
    target = dest[0, :, 0]
    same = target[:, None] == target[None, :]
    earlier = jnp.arange(req_rep)[None, :] < jnp.arange(req_rep)[:, None]
    rank = jnp.sum((same & earlier).astype(jnp.int32), -1)
    slot_of = target * CAP + rank
    buf_rows = lax.axis_size("req") * CAP
    onehot = (slot_of[None, :] == jnp.arange(buf_rows, dtype=jnp.int32)[:, None]).astype(
        jnp.bfloat16
    )
    outbound = jnp.dot(
        onehot, stacked.reshape(req_rep, slot * 2 * per_dev), preferred_element_type=jnp.float32
    )
    outbound = outbound.astype(jnp.bfloat16).reshape(buf_rows, slot, 2, per_dev)
    cache = lax.all_to_all(outbound, "req", split_axis=0, concat_axis=0, tiled=True)
    part = jnp.dot(
        attn.reshape(req_rep * slot, per_dev), w_o, preferred_element_type=jnp.float32
    ).astype(jnp.bfloat16)
    part = lax.optimization_barrier(part)
    total = lax.psum(
        part.astype(jnp.float32).reshape(req_rep, slot, width).astype(jnp.bfloat16), "tp"
    ).astype(jnp.float32)
    mine = lax.dynamic_slice_in_dim(total, lax.axis_index("tp") * req_dev, req_dev, 0)
    hidden_out = (mine + xf).astype(jnp.bfloat16)
    return (hidden_out, cache)


def solution(mesh):
    placed = (
        P(("req", "tp"), None, None),
        P(),
        P(None, "tp"),
        P(None, "tp"),
        P(None, "tp"),
        P("tp", None),
        P("req", None),
        P("req", None, None),
    )
    return jax.shard_map(
        on_device,
        mesh=mesh,
        in_specs=placed,
        out_specs=(P(("req", "tp"), None, None), P("req", None, None, "tp")),
        check_vma=False,
    )
```

profile of v0, /device:TPU:1, one launch (start us, length us, event | category | flops | bytes accessed | tf_op | source)
XLA Modules:
  0.0 276.4 jit_solution(8190934609367659378)
XLA Ops:
  7.2 1.4 fusion.11
  8.6 2.1 fusion.13
  10.8 4.3 %copy.28 = bf16[3072,384]{0,1:T(8,128)(2,1)} copy(bf16[3072,384]{1,0:T(8,128)(2,1)} %param.10) | data formatting | bytes 4718592 | tf_op args[2]
  15.1 4.3 %copy.29 = bf16[3072,384]{0,1:T(8,128)(2,1)} copy(bf16[3072,384]{1,0:T(8,128)(2,1)} %param.11) | data formatting | bytes 4718592 | tf_op args[3]
  20.0 52.5 %all-gather.2.cloned.1.call-done = bf16[32,24,3072]{2,1,0:T(8,128)(2,1)} async-done(((bf16[4,24,3072]{2,1,0:T(8,128)(2,1)}), bf16[32,24,3072]{2,1,0:T(8,128)(2,1)}) %all-gather.2.cloned.1.call-update) | async-done | bytes 4718608 | tf_op jit(solution)/shard_map/all_gather | solution.py:35
  72.5 5.7 %convolution_convert_fusion.3 = bf16[768,384]{1,0:T(8,128)(2,1)S(1)} fusion(bf16[768,3072]{1,0:T(8,128)(2,1)} %bitcast.38, bf16[3072,384]{1,0:T(8,128)(2,1)} %param.12), kind=kOutput, calls=%fused_computation.23 | convolution fusion | flops 1812234240 | bytes 7667712 | tf_op jit(solution)/shard_map/dot_general | solution.py:45
  78.2 1.5 reshape_squeeze_stack_reshape.3
  79.7 5.2 %fusion.1 = f32[32,24,4,96]{3,1,2,0:T(8,128)S(1)} fusion(bf16[4,96,3072,1]{2,1,0,3:T(8,128)(2,1)} %bitcast.35, bf16[32,24,3072]{2,1,0:T(8,128)(2,1)} %all-gather.2.cloned.1.call-done), kind=kOutput, calls=%fused_computation.3 | convolution fusion | flops 1811939328 | bytes 8257536 | tf_op jit(solution)/shard_map/dot_general | solution.py:43
  87.2 2.5 stack_reshape.6
  89.6 1.5 maximum_select_fusion
  91.1 2.2 copy.34
  93.4 2.8 %select_n.23 = bf16[32,18432]{1,0:T(8,128)(2,1)} reshape(bf16[32,24,2,384]{3,2,1,0:T(2,128)(2,1)} %copy.34) | data formatting | bytes 2359296 | tf_op jit(solution)/shard_map/jit(_where)/select_n | solution.py:70
  96.1 5.4 %fusion.3 = f32[32,24,4,96]{3,1,2,0:T(8,128)S(1)} fusion(bf16[4,96,3072,1]{2,1,0,3:T(8,128)(2,1)} %bitcast.34, bf16[32,24,3072]{2,1,0:T(8,128)(2,1)} %all-gather.2.cloned.1.call-done), kind=kOutput, calls=%fused_computation.5 | convolution fusion | flops 1811939328 | bytes 8257536 | tf_op jit(solution)/shard_map/dot_general | solution.py:40
  101.6 2.3 slice_negate_fusion.1
  103.8 4.9 %fusion.25 = (f32[32,4,24]{2,1,0:T(4,128)S(1)}, f32[32,4,24,24]{2,3,1,0:T(8,128)}) fusion(pred[32,24,24]{1,2,0:T(8,128)(4,1)S(1)} %broadcast_and_fusion, bf16[32,24,4,96]{3,1,2,0:T(8,128)(2,1)S(1)} %fusion.9, f32[32,24,4,48]{3,1,2,0:T(8,128)} %get-tuple-element.3, f32[32,24,4,48]{3,1,2,0:T(8,128)} %get-tuple-element.2, f32[32,24,4,96]{3,1,2,0:T(8,128)} %copy-done.1, ...), kind=kOutput, calls=%fused_computation.51 | convolution fusion | flops 15998999 | bytes 3293184 | tf_op jit(solution)/shard_map/sub | solution.py:63
  108.7 2.3 fusion.10
  112.7 5.4 %convolution_convert_fusion.1 = bf16[768,3072]{1,0:T(8,128)(2,1)} fusion(bf16[768,384]{1,0:T(8,128)(2,1)} %reshape_reshape.3, bf16[384,3072]{1,0:T(8,128)(2,1)S(1)} %copy-done), kind=kOutput, calls=%fused_computation.2 | convolution fusion | flops 1814298624 | bytes 7667712 | tf_op jit(solution)/shard_map/dot_general | solution.py:85
  119.4 2.2 convolution_convert_fusion
  121.5 4.6 %reshape.117 = bf16[64,24,2,384]{3,2,1,0:T(2,128)(2,1)} reshape(bf16[64,18432]{1,0:T(8,128)(2,1)} %convolution_convert_fusion) | data formatting | bytes 4718592 | tf_op jit(solution)/shard_map/reshape | solution.py:83
  126.2 7.6 %all-to-all-start = ((bf16[64,24,2,384]{3,2,1,0:T(2,128)(2,1)}), bf16[64,24,2,384]{3,2,1,0:T(2,128)(2,1)}, u32[]{:S(2)}, u32[]{:S(2)}) async-start(bf16[64,24,2,384]{3,2,1,0:T(2,128)(2,1)} %reshape.117), calls=%async_computation | async-start | bytes 4718592 | tf_op jit(solution)/shard_map/all_to_all | solution.py:84
  133.7 61.5 %all-to-all-done = bf16[64,24,2,384]{3,2,1,0:T(2,128)(2,1)} async-done(((bf16[64,24,2,384]{3,2,1,0:T(2,128)(2,1)}), bf16[64,24,2,384]{3,2,1,0:T(2,128)(2,1)}, u32[]{:S(2)}, u32[]{:S(2)}) %all-to-all-start) | async-done | bytes 2359328 | tf_op jit(solution)/shard_map/all_to_all | solution.py:84
  195.3 67.5 %all-reduce.2.cloned.1.call-done = bf16[32,24,3072]{2,1,0:T(8,128)(2,1)} async-done(((bf16[32,24,3072]{2,1,0:T(8,128)(2,1)}), bf16[32,24,3072]{2,1,0:T(8,128)(2,1)}) %all-reduce.2.cloned.1.call-update) | async-done | bytes 4718608 | tf_op jit(solution)/shard_map/psum | solution.py:89
  262.8 2.0 fusion.14
  264.8 4.7 %copy.41 = bf16[64,24,2,384]{3,2,1,0:T(2,128)(2,1)} copy(bf16[64,24,2,384]{3,2,1,0:T(2,128)(2,1)} %all-to-all-done) | data formatting | bytes 4718592
  (32 shorter events, 5.9 us)
Async XLA Ops:
  7.2 105.5 %copy-start = (bf16[384,3072]{1,0:T(8,128)(2,1)S(1)}, bf16[384,3072]{1,0:T(8,128)(2,1)}, u32[]{:S(2)}) copy-start(bf16[384,3072]{1,0:T(8,128)(2,1)} %param.13) | copy-start | bytes 7077892
  7.2 65.3 %all-gather.2.cloned.1.call-start = ((), (), s32[]{:S(2)}) async-start(), calls=%async_computation.1 | async-start | bytes 5308416 | tf_op jit(solution)/shard_map/all_gather | solution.py:35
  10.8 252.0 %all-reduce.2.cloned.1.call-start = ((), (), s32[]{:S(2)}) async-start(), calls=%async_computation.2 | async-start | bytes 9437184 | tf_op jit(solution)/shard_map/psum | solution.py:89
  15.1 4.5 %copy-start.6 = (s32[1,32,1]{1,2,0:T(1,128)S(1)}, s32[1,32,1]{1,2,0:T(1,128)}, u32[]{:S(2)}) copy-start(s32[1,32,1]{1,2,0:T(1,128)} %param.15) | copy-start | bytes 388
  15.1 4.7 %copy-start.5 = (s32[1,32]{1,0:T(1,128)S(1)}, s32[1,32]{1,0:T(1,128)}, u32[]{:S(2)}) copy-start(s32[1,32]{1,0:T(1,128)} %param.14) | copy-start | bytes 388
  78.2 6.7 %copy-start.4 = (bf16[768,384]{1,0:T(8,128)(2,1)}, bf16[768,384]{1,0:T(8,128)(2,1)S(1)}, u32[]{:S(2)}) copy-start(bf16[768,384]{1,0:T(8,128)(2,1)S(1)} %convolution_convert_fusion.3) | copy-start | bytes 1769476
  101.6 2.3 copy-start.1
  118.1 1.3 copy-start.3
  126.2 136.7 %copy-start.2 = (bf16[4,24,3072]{2,1,0:T(8,128)(2,1)S(1)}, bf16[4,24,3072]{2,1,0:T(8,128)(2,1)}, u32[]{:S(2)}) copy-start(bf16[4,24,3072]{2,1,0:T(8,128)(2,1)} %param.8) | copy-start | bytes 1769476
  126.2 69.1 %all-to-all-start = ((bf16[64,24,2,384]{3,2,1,0:T(2,128)(2,1)}), bf16[64,24,2,384]{3,2,1,0:T(2,128)(2,1)}, u32[]{:S(2)}, u32[]{:S(2)}) async-start(bf16[64,24,2,384]{3,2,1,0:T(2,128)(2,1)} %reshape.117), calls=%async_computation | async-start | bytes 4718592 | tf_op jit(solution)/shard_map/all_to_all | solution.py:84
Sparse Core Ops, SparseCore 0:
  10.9 61.5 all-gather.1
  118.2 144.5 all-reduce.1
where the time goes:
time: 277 us; the launch traced here: 276 us
  waiting for transfers between devices  182 us (66%)
  matrix products  31.1 us (11%)
  local copies, waits for them, and re-layouts  30.9 us (11%)
  between operations  14.2 us (5%)
  other arithmetic  11 us (4%)
  starting transfers between devices  7.64 us (3%)
    psum x1, waiting for transfers between devices, on_device(): lax.psum(part.astype(jnp.float32).reshape(req_rep, slot, width).astype(jn...  67.5 us
    all_to_all x1, waiting for transfers between devices, on_device(): lax.all_to_all(outbound, 'req', split_axis=0, concat_axis=0, tiled=True)  61.5 us
    all_gather x1, waiting for transfers between devices, on_device(): piece = lax.all_gather(normed, 'tp', axis=0, tiled=True)  52.5 us
    unnamed x17, local copies, waits for them, and re-layouts  14.5 us
    all_to_all x1, starting transfers between devices, on_device(): lax.all_to_all(outbound, 'req', split_axis=0, concat_axis=0, tiled=True)  7.56 us
    dot_general x1, matrix products, on_device(): values = jnp.dot(flat, w_v, preferred_element_type=jnp.float32)  5.69 us
  transfers between devices with their start and end apart: 3, of which 3 were waited for; matrix products, arithmetic and copies ran while one was open for 6% of the time, Pallas kernels for 0%

commit v1 on v0

--- a/solution.py
+++ b/solution.py
@@ -32,7 +32,9 @@
     xf = hidden_in.astype(jnp.float32)
     mean_sq = jnp.mean(xf * xf, -1, keepdims=True)
     normed = (xf * lax.rsqrt(mean_sq + EPS) * norm_gain).astype(jnp.bfloat16)
-    piece = lax.all_gather(normed, "tp", axis=0, tiled=True)
+    piece = jnp.concatenate(
+        lax.all_to_all(jnp.stack([normed] * lax.axis_size("tp")), "tp", 0, 0), axis=0
+    )
     count = piece.shape[0]
     flat = piece.reshape(count * slot, width)
     shape4 = (count, slot, heads_dev, HD)

time: 277 us -> 329 us (1.19)
  waiting for transfers between devices: 182 us -> 211 us
  starting transfers between devices: 7.64 us -> 25.1 us
    all_to_all x0 -> x1, waiting for transfers between devices: none -> 90.7 us  [on_device(): lax.all_to_all(jnp.stack([normed] * lax.axis_size('tp')), 'tp', 0, 0)]
    all_gather x1 -> x0, waiting for transfers between devices: 52.5 us -> none  [on_device(): piece = lax.all_gather(normed, 'tp', axis=0, tiled=True)]
    all_to_all x0 -> x1, starting transfers between devices: none -> 9.97 us  [on_device(): lax.all_to_all(jnp.stack([normed] * lax.axis_size('tp')), 'tp', 0, 0)]
    all_to_all x1, starting transfers between devices: 7.56 us -> 15.1 us  [on_device(): lax.all_to_all(outbound, 'req', split_axis=0, concat_axis=0, tiled=True)]
    psum x1, waiting for transfers between devices: 67.5 us -> 62.1 us  [on_device(): lax.psum(part.astype(jnp.float32).reshape(req_rep, slot, width).astype(jn...]
    unnamed x17 -> x23, local copies, waits for them, and re-layouts: 14.5 us -> 16.5 us
  transfers between devices with their start and end apart: 3 -> 3, of which waited for: 3 -> 3; matrix products, arithmetic and copies ran while one was open for 6% -> 7% of each run, Pallas kernels for 0% -> 0%
where the time goes in v1:
time: 329 us; the launch traced here: 328 us
  waiting for transfers between devices  211 us (64%)
  local copies, waits for them, and re-layouts  32.6 us (10%)
  matrix products  30.7 us (9%)
  starting transfers between devices  25.1 us (8%)
  other arithmetic  14.2 us (4%)
  between operations  14.2 us (4%)
    all_to_all x1, waiting for transfers between devices, on_device(): lax.all_to_all(jnp.stack([normed] * lax.axis_size('tp')), 'tp', 0, 0)  90.7 us
    psum x1, waiting for transfers between devices, on_device(): lax.psum(part.astype(jnp.float32).reshape(req_rep, slot, width).astype(jn...  62.1 us
    all_to_all x1, waiting for transfers between devices, on_device(): lax.all_to_all(outbound, 'req', split_axis=0, concat_axis=0, tiled=True)  58.4 us
    unnamed x23, local copies, waits for them, and re-layouts  16.5 us
    all_to_all x1, starting transfers between devices, on_device(): lax.all_to_all(outbound, 'req', split_axis=0, concat_axis=0, tiled=True)  15.1 us
    all_to_all x1, starting transfers between devices, on_device(): lax.all_to_all(jnp.stack([normed] * lax.axis_size('tp')), 'tp', 0, 0)  9.97 us
  transfers between devices with their start and end apart: 3, of which 3 were waited for; matrix products, arithmetic and copies ran while one was open for 7% of the time, Pallas kernels for 0%

profile of v1, /device:TPU:1, one launch (start us, length us, event | category | flops | bytes accessed | tf_op | source)
XLA Modules:
  0.0 328.1 jit_solution(13300442189452951738)
XLA Ops:
  9.9 2.8 stack.4
  12.7 10.0 %all-to-all-start = ((bf16[8,4,24,3072]{3,2,1,0:T(8,128)(2,1)}), bf16[8,4,24,3072]{3,2,1,0:T(8,128)(2,1)}, u32[]{:S(2)}, u32[]{:S(2)}) async-start(bf16[8,4,24,3072]{3,2,1,0:T(8,128)(2,1)} %stack.4), calls=%async_computation | async-start | bytes 9437184 | tf_op jit(solution)/shard_map/all_to_all | solution.py:36
  22.6 4.3 %copy.22 = bf16[3072,384]{0,1:T(8,128)(2,1)} copy(bf16[3072,384]{1,0:T(8,128)(2,1)} %param.11) | data formatting | bytes 4718592 | tf_op args[3]
  26.9 4.3 %copy.21 = bf16[3072,384]{0,1:T(8,128)(2,1)} copy(bf16[3072,384]{1,0:T(8,128)(2,1)} %param.10) | data formatting | bytes 4718592 | tf_op args[2]
  31.8 90.7 %all-to-all-done = bf16[8,4,24,3072]{3,2,1,0:T(8,128)(2,1)} async-done(((bf16[8,4,24,3072]{3,2,1,0:T(8,128)(2,1)}), bf16[8,4,24,3072]{3,2,1,0:T(8,128)(2,1)}, u32[]{:S(2)}, u32[]{:S(2)}) %all-to-all-start) | async-done | bytes 4718624 | tf_op jit(solution)/shard_map/all_to_all | solution.py:36
  122.6 5.2 %fusion.25 = f32[32,24,4,96]{3,1,2,0:T(8,128)S(1)} fusion(bf16[32,24,3072,1]{2,1,3,0:T(8,128)(2,1)} %bitcast.4, bf16[4,96,3072,1]{2,1,0,3:T(8,128)(2,1)} %bitcast.35), kind=kOutput, calls=%fused_computation.49 | convolution fusion | flops 1811939328 | bytes 8257536 | tf_op jit(solution)/shard_map/dot_general | solution.py:45
  127.8 2.3 slice_negate_fusion
  131.2 4.5 %fusion.24 = f32[32,24,4,96]{3,1,2,0:T(8,128)S(1)} fusion(bf16[32,24,3072,1]{2,1,3,0:T(8,128)(2,1)} %bitcast.4, bf16[4,96,3072,1]{2,1,0,3:T(8,128)(2,1)S(1)} %bitcast.34), kind=kOutput, calls=%fused_computation.48 | convolution fusion | flops 1811939328 | bytes 8257536 | tf_op jit(solution)/shard_map/dot_general | solution.py:42
  135.7 2.3 slice_negate_fusion.1
  139.1 4.9 %convolution_convert_fusion.3 = bf16[768,384]{1,0:T(8,128)(2,1)S(1)} fusion(bf16[768,3072]{1,0:T(8,128)(2,1)} %bitcast, bf16[3072,384]{1,0:T(8,128)(2,1)S(1)} %copy-done.8), kind=kOutput, calls=%fused_computation.19 | convolution fusion | flops 1812234240 | bytes 7667712 | tf_op jit(solution)/shard_map/dot_general | solution.py:47
  144.0 1.5 reshape_squeeze_stack_reshape.3
  145.5 2.8 fusion.5
  149.6 4.9 %fusion.21 = (f32[32,4,24]{2,1,0:T(4,128)S(1)}, f32[32,4,24,24]{2,3,1,0:T(8,128)}) fusion(pred[32,24,24]{1,2,0:T(8,128)(4,1)S(1)} %broadcast_and_fusion, bf16[32,24,4,96]{3,1,2,0:T(8,128)(2,1)S(1)} %fusion.5, f32[32,24,4,48]{3,1,2,0:T(8,128)} %get-tuple-element.3, f32[32,24,4,48]{3,1,2,0:T(8,128)} %get-tuple-element.2, f32[32,24,4,96]{3,1,2,0:T(8,128)} %copy-done.1, ...), kind=kOutput, calls=%fused_computation.47 | convolution fusion | flops 15998999 | bytes 3293184 | tf_op jit(solution)/shard_map/sub | solution.py:65
  154.5 2.3 fusion.6
  158.4 5.4 %convolution_convert_fusion.1 = bf16[768,3072]{1,0:T(8,128)(2,1)} fusion(bf16[768,384]{1,0:T(8,128)(2,1)} %reshape_reshape.7, bf16[384,3072]{1,0:T(8,128)(2,1)S(1)} %copy-done), kind=kOutput, calls=%fused_computation.2 | convolution fusion | flops 1814298624 | bytes 7667712 | tf_op jit(solution)/shard_map/dot_general | solution.py:87
  166.3 1.5 maximum_select_fusion
  169.0 1.7 select_n.23
  170.8 3.4 %convolution_convert_fusion = bf16[64,18432]{1,0:T(8,128)(2,1)} fusion(bf16[32,18432]{1,0:T(8,128)(2,1)} %select_n.23, s32[32]{0:T(128)S(1)} %multiply_add_fusion), kind=kOutput, calls=%fused_computation.1 | convolution fusion | flops 76679168 | bytes 3539072 | tf_op jit(solution)/shard_map/dot_general | solution.py:82
  174.2 4.6 %reshape.115 = bf16[64,24,2,384]{3,2,1,0:T(2,128)(2,1)} reshape(bf16[64,18432]{1,0:T(8,128)(2,1)} %convolution_convert_fusion) | data formatting | bytes 4718592 | tf_op jit(solution)/shard_map/reshape | solution.py:85
  178.8 15.1 %all-to-all-start.1 = ((bf16[64,24,2,384]{3,2,1,0:T(2,128)(2,1)}), bf16[64,24,2,384]{3,2,1,0:T(2,128)(2,1)}, u32[]{:S(2)}, u32[]{:S(2)}) async-start(bf16[64,24,2,384]{3,2,1,0:T(2,128)(2,1)} %reshape.115), calls=%async_computation.1 | async-start | bytes 4718592 | tf_op jit(solution)/shard_map/all_to_all | solution.py:86
  193.9 58.4 %all-to-all-done.1 = bf16[64,24,2,384]{3,2,1,0:T(2,128)(2,1)} async-done(((bf16[64,24,2,384]{3,2,1,0:T(2,128)(2,1)}), bf16[64,24,2,384]{3,2,1,0:T(2,128)(2,1)}, u32[]{:S(2)}, u32[]{:S(2)}) %all-to-all-start.1) | async-done | bytes 2359328 | tf_op jit(solution)/shard_map/all_to_all | solution.py:86
  252.4 62.1 %all-reduce.2.cloned.1.call-done = bf16[32,24,3072]{2,1,0:T(8,128)(2,1)} async-done(((bf16[32,24,3072]{2,1,0:T(8,128)(2,1)}), bf16[32,24,3072]{2,1,0:T(8,128)(2,1)}) %all-reduce.2.cloned.1.call-update) | async-done | bytes 4718608 | tf_op jit(solution)/shard_map/psum | solution.py:91
  314.5 2.0 fusion.10
  316.5 4.7 %copy.34 = bf16[64,24,2,384]{3,2,1,0:T(2,128)(2,1)} copy(bf16[64,24,2,384]{3,2,1,0:T(2,128)(2,1)} %all-to-all-done.1) | data formatting | bytes 4718592
  (38 shorter events, 12.0 us)
Async XLA Ops:
  7.2 151.3 %copy-start = (bf16[384,3072]{1,0:T(8,128)(2,1)S(1)}, bf16[384,3072]{1,0:T(8,128)(2,1)}, u32[]{:S(2)}) copy-start(bf16[384,3072]{1,0:T(8,128)(2,1)} %param.13) | copy-start | bytes 7077892
  12.7 109.9 %all-to-all-start = ((bf16[8,4,24,3072]{3,2,1,0:T(8,128)(2,1)}), bf16[8,4,24,3072]{3,2,1,0:T(8,128)(2,1)}, u32[]{:S(2)}, u32[]{:S(2)}) async-start(bf16[8,4,24,3072]{3,2,1,0:T(8,128)(2,1)} %stack.4), calls=%async_computation | async-start | bytes 9437184 | tf_op jit(solution)/shard_map/all_to_all | solution.py:36
  22.6 291.9 %all-reduce.2.cloned.1.call-start = ((), (), s32[]{:S(2)}) async-start(), calls=%async_computation.2 | async-start | bytes 9437184 | tf_op jit(solution)/shard_map/psum | solution.py:91
  26.9 4.5 %copy-start.9 = (s32[1,32,1]{1,2,0:T(1,128)S(1)}, s32[1,32,1]{1,2,0:T(1,128)}, u32[]{:S(2)}) copy-start(s32[1,32,1]{1,2,0:T(1,128)} %param.15) | copy-start | bytes 388
  26.9 4.7 %copy-start.7 = (s32[1,32]{1,0:T(1,128)S(1)}, s32[1,32]{1,0:T(1,128)}, u32[]{:S(2)}) copy-start(s32[1,32]{1,0:T(1,128)} %param.14) | copy-start | bytes 388
  127.8 2.4 copy-start.2
  127.8 3.4 %copy-start.5 = (bf16[3072,384]{0,1:T(8,128)(2,1)S(1)}, bf16[3072,384]{0,1:T(8,128)(2,1)}, u32[]{:S(2)}) copy-start(bf16[3072,384]{0,1:T(8,128)(2,1)} %copy.21) | copy-start | bytes 7077892
  135.7 2.4 copy-start.1
  135.7 3.4 %copy-start.8 = (bf16[3072,384]{1,0:T(8,128)(2,1)S(1)}, bf16[3072,384]{1,0:T(8,128)(2,1)}, u32[]{:S(2)}) copy-start(bf16[3072,384]{1,0:T(8,128)(2,1)} %param.12) | copy-start | bytes 7077892
  144.0 1.5 copy-start.6
  163.8 1.1 copy-start.4
  178.8 135.7 %copy-start.3 = (bf16[4,24,3072]{2,1,0:T(8,128)(2,1)S(1)}, bf16[4,24,3072]{2,1,0:T(8,128)(2,1)}, u32[]{:S(2)}) copy-start(bf16[4,24,3072]{2,1,0:T(8,128)(2,1)} %param.8) | copy-start | bytes 1769476
  178.8 73.5 %all-to-all-start.1 = ((bf16[64,24,2,384]{3,2,1,0:T(2,128)(2,1)}), bf16[64,24,2,384]{3,2,1,0:T(2,128)(2,1)}, u32[]{:S(2)}, u32[]{:S(2)}) async-start(bf16[64,24,2,384]{3,2,1,0:T(2,128)(2,1)} %reshape.115), calls=%async_computation.1 | async-start | bytes 4718592 | tf_op jit(solution)/shard_map/all_to_all | solution.py:86
Sparse Core Ops, SparseCore 0:
  164.0 150.4 all-reduce.1
